TPU v7x, 128 devices: a whole 4x4x4 slice. The times are simulated.
128 devices in a mesh: row: 8 (over y_lo, z), col: 16 (over x, y_hi, core).
Axes of the slice: x: 4, y: 4 (y_hi: 2, y_lo: 2; y = y_hi * 2 + y_lo), z: 4, core: 2. Of those that a mesh axis runs over, the one named last changes fastest.
Arguments:
- inverse: float32 [16384, 16384], P('row', 'col'), may hold values from -0.0625 to 0.0625
- pattern: int32 [128, 128], P('row', 'col'), may hold values 0 or 1
- factor_first: float32 [16384, 256], P('col'), may hold values from -1.5 to 1.5
- factor_second: float32 [16384, 256], P('col'), may hold values from -1.5 to 1.5
- rows_first: int32 [64], replicated, may hold values from 0 to 127, as said below
- rows_second: int32 [64], replicated, may hold values from 0 to 127, as said below
- coupling: float32 [256, 256], replicated, may hold values from -0.375 to 0.375
- diag_first: float32 [256, 256], replicated, may hold values from -6 to 6
- diag_second: float32 [256, 256], replicated, may hold values from -6 to 6
Outputs:
- panel_one: float32 [16384, 256], P(('row', 'col'))
- panel_two: float32 [16384, 256], P(('row', 'col'))
- block_one: float32 [256, 256], replicated
- block_cross: float32 [256, 256], replicated
- block_two: float32 [256, 256], replicated
Inputs may be any that keep to these rules, and one draw needn't show every extreme that they name: `rows_first`: 64 distinct block indices in increasing order; the first block, the block 64 and the last block are always among them. `rows_second`: 64 distinct block indices in increasing order; the first block, the block 64 and the last block are always among them.
All inputs are finite; a program needn't handle non-finite values. No bound on the sum of `pattern` on one device may be relied on, other than what follows from the above.
Results may differ from a plain program's by a relative error of at most 0.000071.
Values sent between devices are 32-bit elements; how exact they have to be, the bound alone decides.
A program may use at most 128 MiB of HBM per device.

v0:
```python
import jax
import jax.numpy as jnp
from jax import lax
from jax.sharding import PartitionSpec as P

BLK = 128


def member(block_ids, rows_list):
    hits = (block_ids[:, None] == rows_list[None, :]).astype(jnp.float32)
    return jnp.sum(hits, axis=1)


def per_device(
    inverse,
    pattern,
    factor_first,
    factor_second,
    rows_first,
    rows_second,
    coupling,
    diag_first,
    diag_second,
):
    high = lax.Precision.HIGHEST
    col_count = lax.axis_size("col")
    row_index = lax.axis_index("row")
    col_index = lax.axis_index("col")
    share_rows = factor_first.shape[0]
    local_rows, local_cols = inverse.shape
    quota_rows = local_rows // col_count
    masked = (
        inverse.reshape(local_rows // BLK, BLK, local_cols // BLK, BLK)
        * pattern.astype(jnp.float32)[:, None, :, None]
    ).reshape(local_rows, local_cols)
    share_ids = (col_index * share_rows + jnp.arange(share_rows, dtype=jnp.int32)) // BLK
    own_start = (row_index * col_count + col_index) * quota_rows
    own_ids = (own_start + jnp.arange(quota_rows, dtype=jnp.int32)) // BLK

    def fetch_rows(factor):
        gathered = lax.all_gather(factor, "col", axis=0, tiled=True)
        return lax.dynamic_slice_in_dim(gathered, own_start, quota_rows, 0)

    def panel_product(factor_kept):
        return lax.psum_scatter(
            jnp.dot(masked, factor_kept, precision=high), "col", scatter_dimension=0, tiled=True
        )

    x_one = factor_first * member(share_ids, rows_first)[:, None]
    x_two = factor_second * member(share_ids, rows_second)[:, None]
    panel_one = -panel_product(x_one)
    near_one = fetch_rows(factor_first)
    near_one = near_one * member(own_ids, rows_first)[:, None]
    first_total = lax.psum(jnp.dot(near_one.T, panel_one, precision=high), ("row", "col"))
    block_one = diag_first - first_total
    near_two = fetch_rows(factor_second)
    near_two = near_two * member(own_ids, rows_second)[:, None]
    panel_two = -(panel_product(x_two) + jnp.dot(panel_one, coupling, precision=high))
    cross_sum, quad_sum = lax.psum(
        (
            jnp.dot(panel_one.T, near_two, precision=high),
            jnp.dot(near_two.T, panel_two, precision=high),
        ),
        ("row", "col"),
    )
    block_cross = -(cross_sum + jnp.dot(block_one, coupling, precision=high))
    block_two = diag_second - quad_sum - jnp.dot(coupling.T, block_cross, precision=high)
    return (panel_one, panel_two, block_one, block_cross, block_two)


def solution(mesh):
    return jax.shard_map(
        per_device,
        mesh=mesh,
        in_specs=(
            P("row", "col"),
            P("row", "col"),
            P("col", None),
            P("col", None),
            P(),
            P(),
            P(),
            P(),
            P(),
        ),
        out_specs=(P(("row", "col"), None), P(("row", "col"), None), P(), P(), P()),
        check_vma=False,
    )
```

profile of v0, /device:TPU:1, one launch (start us, length us, event | category | flops | bytes accessed | tf_op | source)
XLA Modules:
  0.0 555.6 jit_solution(4285565588301605714)
XLA Ops:
  7.2 0.7 convert_element_type.15
  8.0 1.0 convert_reduce_fusion
  9.0 0.6 mul.52
  9.6 3.8 copy-done.1
  13.4 0.1 copy-done.2
  13.5 10.3 %fusion.1 = f32[2048,256]{1,0:T(8,128)} fusion(f32[2048,1024]{1,0:T(8,128)S(1)} %copy-done.2, f32[256,8,8,128]{3,2,1,0:T(8,128)S(1)} %bitcast.19, f32[1024,256]{1,0:T(8,128)} %param.11, f32[1024]{0:T(1024)S(1)} %get-tuple-element.6), kind=kOutput, calls=%fused_computation.2 | convolution fusion | flops 6444810240 | bytes 19927040 | tf_op jit(solution)/shard_map/dot_general | solution.py:46
  23.8 0.2 reduce-scatter.5.cloned.1.call-start
  24.1 12.9 %fusion = f32[2048,256]{1,0:T(8,128)} fusion(f32[2048,1024]{1,0:T(8,128)} %param.9, f32[256,8,8,128]{3,2,1,0:T(8,128)} %bitcast.20, f32[1024,256]{1,0:T(8,128)S(1)} %copy-done.3, f32[1024]{0:T(1024)S(1)} %get-tuple-element.5), kind=kOutput, calls=%fused_computation.1 | convolution fusion | flops 6444810240 | bytes 19927040 | tf_op jit(solution)/shard_map/dot_general | solution.py:46
  37.0 0.7 all-gather.5.cloned.1.call-update
  37.8 0.5 all-gather.3.cloned.1.call-update
  38.4 0.1 convert_reduce_fusion.2
  38.5 57.6 %reduce-scatter.3.cloned.1.call-done = f32[128,256]{1,0:T(8,128)} async-done(((f32[2048,256]{1,0:T(8,128)}), f32[128,256]{1,0:T(8,128)}) %reduce-scatter.3.cloned.1.call-update) | async-done | bytes 131088 | tf_op jit(solution)/shard_map/reduce_scatter | solution.py:45
  96.1 0.9 neg.9
  97.0 73.0 %reduce-scatter.5.cloned.1.call-done = f32[128,256]{1,0:T(8,128)} async-done(((f32[2048,256]{1,0:T(8,128)}), f32[128,256]{1,0:T(8,128)}) %reduce-scatter.5.cloned.1.call-update) | async-done | bytes 131088 | tf_op jit(solution)/shard_map/reduce_scatter | solution.py:45
  170.0 1.2 fusion.4
  171.2 112.4 %all-gather.5.cloned.1.call-done = f32[16384,256]{1,0:T(8,128)} async-done(((f32[1024,256]{1,0:T(8,128)}), f32[16384,256]{1,0:T(8,128)}) %all-gather.5.cloned.1.call-update) | async-done | bytes 16777232 | tf_op jit(solution)/shard_map/all_gather | solution.py:41
  283.5 2.1 fusion.13
  285.6 2.1 fusion.12
  287.7 105.6 %all-gather.3.cloned.1.call-done = f32[16384,256]{1,0:T(8,128)} async-done(((f32[1024,256]{1,0:T(8,128)}), f32[16384,256]{1,0:T(8,128)}) %all-gather.3.cloned.1.call-update) | async-done | bytes 16777232 | tf_op jit(solution)/shard_map/all_gather | solution.py:41
  393.3 2.1 fusion.9
  395.4 148.9 %all-reduce.3.cloned.1.call-done = (f32[256,256]{1,0:T(8,128)}, f32[256,256]{1,0:T(8,128)}, f32[256,256]{1,0:T(8,128)}) async-done(((f32[256,256]{1,0:T(8,128)}, f32[256,256]{1,0:T(8,128)}, f32[256,256]{1,0:T(8,128)}), (f32[256,256]{1,0:T(8,128)}, f32[256,256]{1,0:T(8,128)}, f32[256,256]{1,0:T(8,128)})) %all-reduce.3.cloned.1.call-update) | async-done | bytes 786448 | tf_op jit(solution)/shard_map/psum | solution.py:54
  544.3 1.0 sub.23
  545.3 1.4 fusion.3
  546.7 2.3 fusion.2
  (32 shorter events, 0.4 us)
Async XLA Ops:
  7.2 162.8 %copy-start = (f32[256,256]{1,0:T(8,128)S(1)}, f32[256,256]{1,0:T(8,128)}, u32[]{:S(2)}) copy-start(f32[256,256]{1,0:T(8,128)} %param.15) | copy-start | bytes 786436
  7.2 88.9 %reduce-scatter.3.cloned.1.call-start = ((), (), s32[]{:S(2)}) async-start(), calls=%async_computation.2 | async-start | bytes 2228224 | tf_op jit(solution)/shard_map/reduce_scatter | solution.py:45
  8.0 5.5 copy-start.2
  9.6 3.8 copy-start.1
  13.5 10.5 %copy-start.3 = (f32[1024,256]{1,0:T(8,128)S(1)}, f32[1024,256]{1,0:T(8,128)}, u32[]{:S(2)}) copy-start(f32[1024,256]{1,0:T(8,128)} %param.12) | copy-start | bytes 3145732
  23.8 146.2 %reduce-scatter.5.cloned.1.call-start = ((), (), s32[]{:S(2)}) async-start(), calls=%async_computation.3 | async-start | bytes 2228224 | tf_op jit(solution)/shard_map/reduce_scatter | solution.py:45
  24.0 14.3 %copy-start.10 = (s32[64]{0:T(128)S(1)}, s32[64]{0:T(128)}, u32[]{:S(2)}) copy-start(s32[64]{0:T(128)} %param.14) | copy-start | bytes 772
  24.0 14.3 %copy-start.11 = (s32[64]{0:T(128)S(1)}, s32[64]{0:T(128)}, u32[]{:S(2)}) copy-start(s32[64]{0:T(128)} %param.13) | copy-start | bytes 772
  24.1 520.2 %copy-start.8 = (f32[256,256]{1,0:T(8,128)S(1)}, f32[256,256]{1,0:T(8,128)}, u32[]{:S(2)}) copy-start(f32[256,256]{1,0:T(8,128)} %param.16) | copy-start | bytes 786436
  36.9 509.8 %copy-start.9 = (f32[256,256]{1,0:T(8,128)S(1)}, f32[256,256]{1,0:T(8,128)}, u32[]{:S(2)}) copy-start(f32[256,256]{1,0:T(8,128)} %param.17) | copy-start | bytes 786436
  37.0 246.6 %all-gather.5.cloned.1.call-start = ((), (), s32[]{:S(2)}) async-start(), calls=%async_computation.5 | async-start | bytes 17825792 | tf_op jit(solution)/shard_map/all_gather | solution.py:41
  37.7 355.5 %all-gather.3.cloned.1.call-start = ((), (), s32[]{:S(2)}) async-start(), calls=%async_computation.4 | async-start | bytes 17825792 | tf_op jit(solution)/shard_map/all_gather | solution.py:41
  38.3 506.0 %all-reduce.3.cloned.1.call-start = ((), (), s32[]{:S(2)}) async-start(), calls=%async_computation.6 | async-start | bytes 1572864 | tf_op jit(solution)/shard_map/psum | solution.py:54
  97.0 452.1 %copy-start.4 = (f32[128,256]{1,0:T(8,128)}, f32[128,256]{1,0:T(8,128)S(1)}, u32[]{:S(2)}) copy-start(f32[128,256]{1,0:T(8,128)S(1)} %neg.9) | copy-start | bytes 393220
  171.2 377.9 %copy-start.7 = (f32[128,256]{1,0:T(8,128)}, f32[128,256]{1,0:T(8,128)S(1)}, u32[]{:S(2)}) copy-start(f32[128,256]{1,0:T(8,128)S(1)} %fusion.4) | copy-start | bytes 393220
  545.2 3.8 copy-start.5
  546.7 2.4 copy-start.6
Sparse Core Ops, SparseCore 0:
  23.9 72.0 reduce-scatter.2
  100.0 69.9 reduce-scatter.4
  172.4 111.1 all-gather.4
  285.8 107.4 all-gather.2
  398.7 145.5 all-reduce.2
where the time goes:
time: 556 us
  waiting for transfers between devices  499 us (90%)
  matrix products  34.3 us (6%)
  between operations  14 us (3%)
    all_gather x2, waiting for transfers between devices, fetch_rows(): gathered = lax.all_gather(factor, 'col', axis=0, tiled=True)  218 us
    psum x1, waiting for transfers between devices, per_device(): lax.psum(jnp.dot(near_one.T, panel_one, precision=high), ('row', 'col'))  149 us
    reduce_scatter x2, waiting for transfers between devices, panel_product(): lax.psum_scatter(jnp.dot(masked, factor_kept, precision=high), 'col', sca...  131 us
    dot_general x2, matrix products, panel_product(): jnp.dot(masked, factor_kept, precision=high)  23.1 us
  transfers between devices with their start and end apart: 5, of which 5 were waited for; matrix products, arithmetic and copies ran while one was open for 3% of the time, Pallas kernels for 0%

commit v1 on v0

--- a/solution.py
+++ b/solution.py
@@ -4,6 +4,11 @@
 from jax.sharding import PartitionSpec as P
 
 BLK = 128
+
+
+def axis_by_axis(array, inner_axis, outer_axis):
+    inner = lax.psum(array, inner_axis)
+    return lax.psum(inner, outer_axis)
 
 
 def member(block_ids, rows_list):
@@ -51,7 +56,7 @@
     panel_one = -panel_product(x_one)
     near_one = fetch_rows(factor_first)
     near_one = near_one * member(own_ids, rows_first)[:, None]
-    first_total = lax.psum(jnp.dot(near_one.T, panel_one, precision=high), ("row", "col"))
+    first_total = axis_by_axis(jnp.dot(near_one.T, panel_one, precision=high), "col", "row")
     block_one = diag_first - first_total
     near_two = fetch_rows(factor_second)
     near_two = near_two * member(own_ids, rows_second)[:, None]

time: 556 us -> 773 us (1.39)
  waiting for transfers between devices: 499 us -> 715 us
    psum x1 -> x3, waiting for transfers between devices: 149 us -> 362 us  [the longest x1 156 us: per_device(): lax.psum((jnp.dot(panel_one.T, near_two, precision=high), jnp.dot(near_tw...]
    all_gather x2, waiting for transfers between devices: 218 us -> 226 us  [fetch_rows(): gathered = lax.all_gather(factor, 'col', axis=0, tiled=True)]
  transfers between devices with their start and end apart: 5 -> 7, of which waited for: 5 -> 7; matrix products, arithmetic and copies ran while one was open for 3% -> 3% of each run, Pallas kernels for 0% -> 0%
where the time goes in v1:
time: 773 us
  waiting for transfers between devices  715 us (92%)
  matrix products  34.1 us (4%)
  between operations  14.3 us (2%)
    all_gather x2, waiting for transfers between devices, fetch_rows(): gathered = lax.all_gather(factor, 'col', axis=0, tiled=True)  226 us
    psum x1, waiting for transfers between devices, per_device(): lax.psum((jnp.dot(panel_one.T, near_two, precision=high), jnp.dot(near_tw...  156 us
    psum x1, waiting for transfers between devices, axis_by_axis(): inner = lax.psum(array, inner_axis)  141 us
    reduce_scatter x2, waiting for transfers between devices, panel_product(): lax.psum_scatter(jnp.dot(masked, factor_kept, precision=high), 'col', sca...  126 us
    psum x1, waiting for transfers between devices, axis_by_axis(): return lax.psum(inner, outer_axis)  65.2 us
    dot_general x2, matrix products, panel_product(): jnp.dot(masked, factor_kept, precision=high)  23.1 us
  transfers between devices with their start and end apart: 7, of which 7 were waited for; matrix products, arithmetic and copies ran while one was open for 3% of the time, Pallas kernels for 0%

profile of v1, /device:TPU:1, one launch (start us, length us, event | category | flops | bytes accessed | tf_op | source)
XLA Modules:
  0.0 772.6 jit_solution(5722496783620294308)
XLA Ops:
  7.2 0.7 convert_element_type.15
  8.0 1.0 convert_reduce_fusion
  9.0 0.6 mul.52
  9.6 3.8 copy-done.1
  13.5 10.3 %fusion.1 = f32[2048,256]{1,0:T(8,128)} fusion(f32[2048,1024]{1,0:T(8,128)S(1)} %copy-done.2, f32[256,8,8,128]{3,2,1,0:T(8,128)S(1)} %bitcast.19, f32[1024,256]{1,0:T(8,128)} %param.11, f32[1024]{0:T(1024)S(1)} %get-tuple-element.6), kind=kOutput, calls=%fused_computation.2 | convolution fusion | flops 6444810240 | bytes 19927040 | tf_op jit(solution)/shard_map/dot_general | solution.py:51
  23.8 0.7 all-gather.3.cloned.1.call-update
  24.5 0.2 reduce-scatter.5.cloned.1.call-start
  24.8 12.8 %fusion = f32[2048,256]{1,0:T(8,128)} fusion(f32[2048,1024]{1,0:T(8,128)} %param.9, f32[256,8,8,128]{3,2,1,0:T(8,128)} %bitcast.20, f32[1024,256]{1,0:T(8,128)S(1)} %copy-done.3, f32[1024]{0:T(1024)S(1)} %get-tuple-element.5), kind=kOutput, calls=%fused_computation.1 | convolution fusion | flops 6444810240 | bytes 19927040 | tf_op jit(solution)/shard_map/dot_general | solution.py:51
  37.8 58.2 %reduce-scatter.3.cloned.1.call-done = f32[128,256]{1,0:T(8,128)} async-done(((f32[2048,256]{1,0:T(8,128)}), f32[128,256]{1,0:T(8,128)}) %reduce-scatter.3.cloned.1.call-update) | async-done | bytes 131088 | tf_op jit(solution)/shard_map/reduce_scatter | solution.py:50
  96.0 0.9 neg.9
  96.9 112.6 %all-gather.3.cloned.1.call-done = f32[16384,256]{1,0:T(8,128)} async-done(((f32[1024,256]{1,0:T(8,128)}), f32[16384,256]{1,0:T(8,128)}) %all-gather.3.cloned.1.call-update) | async-done | bytes 16777232 | tf_op jit(solution)/shard_map/all_gather | solution.py:46
  209.6 2.1 fusion.9
  211.7 0.5 all-gather.5.cloned.1.call-update
  212.3 67.4 %reduce-scatter.5.cloned.1.call-done = f32[128,256]{1,0:T(8,128)} async-done(((f32[2048,256]{1,0:T(8,128)}), f32[128,256]{1,0:T(8,128)}) %reduce-scatter.5.cloned.1.call-update) | async-done | bytes 131088 | tf_op jit(solution)/shard_map/reduce_scatter | solution.py:50
  279.8 1.2 fusion.4
  281.0 141.4 %all-reduce.5.cloned.1.call-done = f32[256,256]{1,0:T(8,128)} async-done(((f32[256,256]{1,0:T(8,128)}), f32[256,256]{1,0:T(8,128)}) %all-reduce.5.cloned.1.call-update) | async-done | bytes 262160 | tf_op jit(solution)/shard_map/psum | solution.py:10
  422.5 113.5 %all-gather.5.cloned.1.call-done = f32[16384,256]{1,0:T(8,128)} async-done(((f32[1024,256]{1,0:T(8,128)}), f32[16384,256]{1,0:T(8,128)}) %all-gather.5.cloned.1.call-update) | async-done | bytes 16777232 | tf_op jit(solution)/shard_map/all_gather | solution.py:46
  536.0 2.1 fusion.13
  538.0 2.1 fusion.12
  540.1 65.2 %all-reduce.7.cloned.1.call-done = f32[256,256]{1,0:T(8,128)} async-done(((f32[256,256]{1,0:T(8,128)}), f32[256,256]{1,0:T(8,128)}) %all-reduce.7.cloned.1.call-update) | async-done | bytes 262160 | tf_op jit(solution)/shard_map/psum | solution.py:11
  605.4 1.0 sub.23
  606.4 155.6 %all-reduce.9.cloned.1.call-done = (f32[256,256]{1,0:T(8,128)}, f32[256,256]{1,0:T(8,128)}) async-done(((f32[256,256]{1,0:T(8,128)}, f32[256,256]{1,0:T(8,128)}), (f32[256,256]{1,0:T(8,128)}, f32[256,256]{1,0:T(8,128)})) %all-reduce.9.cloned.1.call-update) | async-done | bytes 524304 | tf_op jit(solution)/shard_map/psum | solution.py:64
  762.0 1.3 fusion.3
  763.3 2.3 fusion.2
  (38 shorter events, 0.7 us)
Async XLA Ops:
  7.2 272.6 %copy-start = (f32[256,256]{1,0:T(8,128)S(1)}, f32[256,256]{1,0:T(8,128)}, u32[]{:S(2)}) copy-start(f32[256,256]{1,0:T(8,128)} %param.15) | copy-start | bytes 786436
  7.2 88.8 %reduce-scatter.3.cloned.1.call-start = ((), (), s32[]{:S(2)}) async-start(), calls=%async_computation.2 | async-start | bytes 2228224 | tf_op jit(solution)/shard_map/reduce_scatter | solution.py:50
  8.0 5.5 copy-start.2
  9.6 3.8 copy-start.1
  13.5 11.3 %copy-start.3 = (f32[1024,256]{1,0:T(8,128)S(1)}, f32[1024,256]{1,0:T(8,128)}, u32[]{:S(2)}) copy-start(f32[1024,256]{1,0:T(8,128)} %param.12) | copy-start | bytes 3145732
  23.8 185.8 %all-gather.3.cloned.1.call-start = ((), (), s32[]{:S(2)}) async-start(), calls=%async_computation.4 | async-start | bytes 17825792 | tf_op jit(solution)/shard_map/all_gather | solution.py:46
  24.5 255.2 %reduce-scatter.5.cloned.1.call-start = ((), (), s32[]{:S(2)}) async-start(), calls=%async_computation.3 | async-start | bytes 2228224 | tf_op jit(solution)/shard_map/reduce_scatter | solution.py:50
  24.8 12.9 %copy-start.10 = (s32[64]{0:T(128)S(1)}, s32[64]{0:T(128)}, u32[]{:S(2)}) copy-start(s32[64]{0:T(128)} %param.14) | copy-start | bytes 772
  24.8 12.9 %copy-start.11 = (s32[64]{0:T(128)S(1)}, s32[64]{0:T(128)}, u32[]{:S(2)}) copy-start(s32[64]{0:T(128)} %param.13) | copy-start | bytes 772
  24.8 580.6 %copy-start.8 = (f32[256,256]{1,0:T(8,128)S(1)}, f32[256,256]{1,0:T(8,128)}, u32[]{:S(2)}) copy-start(f32[256,256]{1,0:T(8,128)} %param.16) | copy-start | bytes 786436
  37.6 725.7 %copy-start.9 = (f32[256,256]{1,0:T(8,128)S(1)}, f32[256,256]{1,0:T(8,128)}, u32[]{:S(2)}) copy-start(f32[256,256]{1,0:T(8,128)} %param.17) | copy-start | bytes 786436
  37.6 384.8 %all-reduce.5.cloned.1.call-start = ((), (), s32[]{:S(2)}) async-start(), calls=%async_computation.5 | async-start | bytes 524288 | tf_op jit(solution)/shard_map/psum | solution.py:10
  96.9 668.8 %copy-start.4 = (f32[128,256]{1,0:T(8,128)}, f32[128,256]{1,0:T(8,128)S(1)}, u32[]{:S(2)}) copy-start(f32[128,256]{1,0:T(8,128)S(1)} %neg.9) | copy-start | bytes 393220
  211.7 324.3 %all-gather.5.cloned.1.call-start = ((), (), s32[]{:S(2)}) async-start(), calls=%async_computation.7 | async-start | bytes 17825792 | tf_op jit(solution)/shard_map/all_gather | solution.py:46
  212.3 393.1 %all-reduce.7.cloned.1.call-start = ((), (), s32[]{:S(2)}) async-start(), calls=%async_computation.6 | async-start | bytes 524288 | tf_op jit(solution)/shard_map/psum | solution.py:11
  281.0 484.7 %copy-start.7 = (f32[128,256]{1,0:T(8,128)}, f32[128,256]{1,0:T(8,128)S(1)}, u32[]{:S(2)}) copy-start(f32[128,256]{1,0:T(8,128)S(1)} %fusion.4) | copy-start | bytes 393220
  422.4 339.6 %all-reduce.9.cloned.1.call-start = ((), (), s32[]{:S(2)}) async-start(), calls=%async_computation.8 | async-start | bytes 1048576 | tf_op jit(solution)/shard_map/psum | solution.py:64
  606.3 159.3 %copy-start.5 = (f32[256,256]{1,0:T(8,128)}, f32[256,256]{1,0:T(8,128)S(1)}, u32[]{:S(2)}) copy-start(f32[256,256]{1,0:T(8,128)S(1)} %sub.23) | copy-start | bytes 786436
  763.3 2.4 copy-start.6
Sparse Core Ops, SparseCore 0:
  23.9 72.0 reduce-scatter.2
  98.4 111.1 all-gather.2
  213.5 66.1 reduce-scatter.4
  282.7 139.6 all-reduce.4
  424.6 111.2 all-gather.4
  538.3 67.0 all-reduce.6
  610.9 151.0 all-reduce.8
